TPU v7x, 1024 devices: a whole 4x8x16 slice. The times are simulated.
1024 devices in a mesh: row: 16 (over z), col: 64 (over y, x, core).
Axes of the slice: x: 4, y: 8, z: 16, core: 2. Of those that a mesh axis runs over, the one named last changes fastest.
Arguments:
- slot_factors: bfloat16 [16, 64, 2, 1024, 256], P('row', 'col'), may hold values from -0.75 to 0.75
- slot_pairs: int32 [16, 64, 2], P('row', 'col'), may hold values from 0 to 2, as said below
- pivot_factors: bfloat16 [32, 1024, 256], P('row', 'col'), may hold values from -0.75 to 0.75
- a_factors: bfloat16 [64, 1024, 256], P('col'), as said below
- diag_factor: float32 [1024, 1024], replicated, as said below
- sketch: float32 [1024, 128], replicated, as said below
Outputs:
- panel_basis: float32 [64, 1024, 128], P('col')
- panel_coeff: float32 [64, 1024, 128], P('col')
Inputs may be any that keep to these rules, and one draw needn't show every extreme that they name: `slot_pairs`: on each cell (r, c) the live codes come first, are distinct and below 2; the remaining entries equal 2. Every cell has at least one live slot, and in every draw some cell is full and some cell has exactly one. `diag_factor`: lower triangular; the diagonal lies between 1 and 2. `a_factors`: real values of order one. `sketch`: real values.
All inputs are finite; a program needn't handle non-finite values.
Results may differ from a plain program's by a relative error of at most 0.0003.
Values may be sent and summed in bfloat16 or wider, within the bound.
No kernel may reach another device: no remote copies, remote signals or barrier semaphores. Data moves between devices by JAX's collectives and lax.ppermute only.
A program may use at most 64 MiB of HBM per device.

v0:
```python
import jax
import jax.numpy as jnp
from jax import lax
from jax.sharding import PartitionSpec as P


def orthonormal_rows(sketch_rows, gram_matrix):
    factor_low = jnp.linalg.cholesky(gram_matrix)
    solved = lax.linalg.triangular_solve(
        factor_low, jnp.swapaxes(sketch_rows, 1, 2), left_side=True, lower=True
    )
    return jnp.swapaxes(solved, 1, 2)


def shards(slot_factors, slot_pairs, pivot_factors, a_factors, diag_factor, sketch):
    precise_mode = lax.Precision.HIGHEST
    tile_size = sketch.shape[0]
    rank_size = sketch.shape[1]
    tile_rows = a_factors.shape[0]
    earlier = pivot_factors.shape[0]
    pivot_data = lax.all_gather(pivot_factors, "col", axis=1, tiled=True).astype(jnp.float32)
    pivot_left_factor = pivot_data[..., :rank_size]
    pivot_right_factor = pivot_data[..., rank_size:]
    weights = jnp.einsum("jbr,bc->jrc", pivot_left_factor, sketch, precision=precise_mode)
    slot_data = slot_factors[0, 0].astype(jnp.float32)
    slot_left_factor = slot_data[..., :rank_size]
    slot_right_factor = slot_data[..., rank_size:]
    pair_codes = slot_pairs[0, 0]
    tile_selector = jax.nn.one_hot(pair_codes // earlier, tile_rows, dtype=jnp.float32)
    column_selector = jax.nn.one_hot(pair_codes % earlier, earlier, dtype=jnp.float32)
    slot_pivot_right_factor = jnp.einsum(
        "kf,fed->ked", column_selector, pivot_right_factor, precision=precise_mode
    )
    coupling_matrix = jnp.einsum(
        "jzk,jzu->jku", slot_right_factor, slot_pivot_right_factor, precision=precise_mode
    )
    slot_weights = jnp.einsum("sj,jrc->src", column_selector, weights, precision=precise_mode)
    panel_kernel = jnp.einsum("src,scd->srd", coupling_matrix, slot_weights, precision=precise_mode)
    update_contribution = jnp.einsum(
        "gxn,gny->gxy", slot_left_factor, panel_kernel, precision=precise_mode
    )
    y_part = jnp.einsum("st,sbd->tbd", tile_selector, update_contribution, precision=precise_mode)
    a_data = a_factors.astype(jnp.float32)
    a_left = a_data[..., :rank_size]
    a_right = a_data[..., rank_size:]
    a_sketch = jnp.einsum("ibr,bc->irc", a_right, sketch, precision=precise_mode)
    y_a = jnp.einsum("ibr,irc->ibc", a_left, a_sketch, precision=precise_mode)
    sketch_rows = y_a - lax.psum(y_part, "row")
    gram_matrix = jnp.einsum("ibr,ibc->irc", sketch_rows, sketch_rows, precision=precise_mode)
    basis_column_count = orthonormal_rows(sketch_rows, gram_matrix)
    slot_basis_matrix = jnp.einsum(
        "hw,wlf->hlf", tile_selector, basis_column_count, precision=precise_mode
    )
    slot_pivot_left_factor = jnp.einsum(
        "kf,fed->ked", column_selector, pivot_left_factor, precision=precise_mode
    )
    inner_product = jnp.einsum(
        "jzk,jzu->jku", slot_left_factor, slot_basis_matrix, precision=precise_mode
    )
    reduced = jnp.einsum("src,srd->scd", coupling_matrix, inner_product, precision=precise_mode)
    lifted = jnp.einsum("sbc,scd->sbd", slot_pivot_left_factor, reduced, precision=precise_mode)
    m_part = jnp.einsum("st,sbd->tbd", tile_selector, lifted, precision=precise_mode)
    m_sum = lax.psum(m_part, "row")
    a_inner = jnp.einsum("ibr,ibc->irc", a_left, basis_column_count, precision=precise_mode)
    m_a = jnp.einsum("ibr,irc->ibc", a_right, a_inner, precision=precise_mode)
    projected = m_a - m_sum
    stacked = jnp.transpose(projected, (1, 0, 2)).reshape(tile_size, tile_rows * rank_size)
    solved = lax.linalg.triangular_solve(diag_factor, stacked, left_side=True, lower=True)
    coefficient = jnp.transpose(solved.reshape(tile_size, tile_rows, rank_size), (1, 0, 2))
    root_tile = jnp.sqrt(jnp.float32(tile_size))
    return (basis_column_count * root_tile, coefficient / root_tile)


def solution(mesh):
    in_specs = (
        P("row", "col", None, None, None),
        P("row", "col", None),
        P("row", "col", None),
        P("col", None, None),
        P(),
        P(),
    )
    out_specs = (P("col", None, None), P("col", None, None))
    return jax.shard_map(shards, mesh=mesh, in_specs=in_specs, out_specs=out_specs, check_vma=False)
```

profile of v0, /device:TPU:6, one launch (start us, length us, event | category | flops | bytes accessed | tf_op | source)
XLA Modules:
  0.0 455.1 jit_solution(4225580014934715081)
XLA Ops:
  10.0 4.7 %fusion = f32[1024,1024]{1,0:T(8,128)} fusion(f32[1024,1024]{1,0:T(8,128)} %param.10), kind=kLoop, calls=%fused_computation.3 | loop fusion | flops 2097152 | bytes 8388608 | tf_op jit(solution)/shard_map/triangular_solve | solution.py:68
  14.7 91.6 %all-gather.2.cloned.1.call-done = bf16[2,1024,256]{2,1,0:T(8,128)(2,1)} async-done(((bf16[2,16,256]{2,1,0:T(8,128)(2,1)}), bf16[2,1024,256]{2,1,0:T(8,128)(2,1)}) %all-gather.2.cloned.1.call-update) | async-done | bytes 1048592 | tf_op jit(solution)/shard_map/all_gather | solution.py:21
  106.3 1.7 fusion.19
  108.5 1.3 fusion.85
  111.9 1.4 fusion.2
  114.1 1.7 fusion.23
  115.8 142.1 %all-reduce.3.cloned.1.call-done = f32[1,1024,128]{1,2,0:T(8,128)} async-done(((f32[1,1024,128]{1,2,0:T(8,128)}), f32[1,1024,128]{1,2,0:T(8,128)}) %all-reduce.3.cloned.1.call-update) | async-done | bytes 524304 | tf_op jit(solution)/shard_map/psum | solution.py:48
  257.9 1.5 fusion.3
  260.1 11.7 %custom-call.10 = f32[1,128,128]{2,1,0:T(8,128)S(1)} custom-call(f32[1,128,128]{2,1,0:T(8,128)S(1)} %fusion.73), custom_call_target="Cholesky" | custom-call | tf_op jit(solution)/shard_map/jit(cholesky)/cholesky | solution.py:8
  273.2 9.8 %custom-call.11 = f32[1,1,128,128]{2,3,1,0:T(8,128)S(1)} custom-call(f32[1,1,128,128]{3,2,1,0:T(8,128)S(1)} %fusion.64), custom_call_target="InvertDiagBlocksLowerTriangular" | custom-call | tf_op jit(solution)/shard_map/triangular_solve | solution.py:9
  283.8 1.1 fusion.10
  285.3 2.2 fusion.6
  287.6 2.7 fusion.12
  291.4 27.7 %while.1 = (s32[]{:T(128)}, f32[1024,1024]{1,0:T(8,128)}, s32[8,2]{0,1:T(2,128)S(1)}, f32[8,128,128]{2,1,0:T(8,128)}, s32[]{:T(128)}) while((s32[]{:T(128)}, f32[1024,1024]{1,0:T(8,128)}, s32[8,2]{0,1:T(2,128)S(1)}, f32[8,128,128]{2,1,0:T(8,128)}, s32[]{:T(128)}) %tuple.44), condition=%wide.while_cond, body=%wide.while_body.sunk | while | flops 2 | bytes 132205 | solution.py:68
  292.0 2.8 bitcast_dynamic-update-slice_fusion.9
  295.5 2.8 bitcast_dynamic-update-slice_fusion.9
  299.0 2.8 bitcast_dynamic-update-slice_fusion.9
  302.4 2.8 bitcast_dynamic-update-slice_fusion.9
  305.9 2.8 bitcast_dynamic-update-slice_fusion.9
  309.4 2.8 bitcast_dynamic-update-slice_fusion.9
  312.8 2.8 bitcast_dynamic-update-slice_fusion.9
  316.3 2.7 bitcast_dynamic-update-slice_fusion.9
  319.0 79.4 %custom-call.12 = f32[8,128,128]{1,2,0:T(8,128)S(1)} custom-call(f32[8,128,128]{2,1,0:T(8,128)} %get-tuple-element.9), custom_call_target="InvertDiagBlocksLowerTriangular" | custom-call | tf_op jit(solution)/shard_map/triangular_solve | solution.py:68
  399.8 33.2 %all-reduce.5.cloned.1.call-done = f32[1,1024,128]{1,2,0:T(8,128)} async-done(((f32[1,1024,128]{1,2,0:T(8,128)}), f32[1,1024,128]{1,2,0:T(8,128)}) %all-reduce.5.cloned.1.call-update) | async-done | bytes 524304 | tf_op jit(solution)/shard_map/psum | solution.py:63
  433.0 1.4 fusion.4
  434.7 1.1 convolution_subtract_fusion.4
  436.2 1.3 convolution_subtract_fusion.3
  437.8 1.4 convolution_subtract_fusion.6
  439.5 1.5 convolution_subtract_fusion.5
  441.4 1.7 convolution_subtract_fusion.2
  443.4 1.8 convolution_subtract_fusion.1
  445.5 1.9 convolution_subtract_fusion
  (71 shorter events, 20.1 us)
Async XLA Ops:
  7.2 99.1 %copy-start = (f32[1024,128]{1,0:T(8,128)S(1)}, f32[1024,128]{1,0:T(8,128)}, u32[]{:S(2)}) copy-start(f32[1024,128]{1,0:T(8,128)} %param.11) | copy-start | bytes 1572868
  7.2 99.1 %all-gather.2.cloned.1.call-start = ((), (), s32[]{:S(2)}) async-start(), calls=%async_computation | async-start | bytes 1064960 | tf_op jit(solution)/shard_map/all_gather | solution.py:21
  7.9 250.0 %all-reduce.3.cloned.1.call-start = ((), (), s32[]{:S(2)}) async-start(), calls=%async_computation.1 | async-start | bytes 1048576 | tf_op jit(solution)/shard_map/psum | solution.py:48
  14.7 95.8 %copy-start.1 = (bf16[1,1,2,1024,256]{4,3,2,1,0:T(8,128)(2,1)S(1)}, bf16[1,1,2,1024,256]{4,3,2,1,0:T(8,128)(2,1)}, u32[]{:S(2)}) copy-start(bf16[1,1,2,1024,256]{4,3,2,1,0:T(8,128)(2,1)} %param.6) | copy-start | bytes 3145732
  108.0 5.6 %copy-start.2 = (bf16[1,1024,256]{2,1,0:T(8,128)(2,1)S(1)}, bf16[1,1024,256]{2,1,0:T(8,128)(2,1)}, u32[]{:S(2)}) copy-start(bf16[1,1024,256]{2,1,0:T(8,128)(2,1)} %param.9) | copy-start | bytes 1572868
  113.4 319.6 %all-reduce.5.cloned.1.call-start = ((), (), s32[]{:S(2)}) async-start(), calls=%async_computation.2 | async-start | bytes 1048576 | tf_op jit(solution)/shard_map/psum | solution.py:63
  115.8 171.7 %copy-start.4 = (s32[1,1,2]{2,1,0:T(1,128)S(1)}, s32[1,1,2]{2,1,0:T(1,128)}, u32[]{:S(2)}) copy-start(s32[1,1,2]{2,1,0:T(1,128)} %param.7) | copy-start | bytes 28
  284.9 114.5 %copy-start.3 = (bf16[1,1024,256]{2,1,0:T(8,128)(2,1)S(1)}, bf16[1,1024,256]{2,1,0:T(8,128)(2,1)}, u32[]{:S(2)}) copy-start(bf16[1,1024,256]{2,1,0:T(8,128)(2,1)} %param.9) | copy-start | bytes 1572868
Sparse Core Ops, SparseCore 0:
  12.4 93.8 all-gather.1
  113.5 144.3 all-reduce.2
  291.5 141.4 all-reduce.4
where the time goes:
time: 456 us; the launch traced here: 455 us
  waiting for transfers between devices  268 us (59%)
  other arithmetic  110 us (24%)
  matrix products  31.9 us (7%)
  local copies, waits for them, and re-layouts  31.4 us (7%)
  between operations  14.1 us (3%)
    psum x1, waiting for transfers between devices, shards(): sketch_rows = y_a - lax.psum(y_part, 'row')  142 us
    all_gather x1, waiting for transfers between devices, shards(): lax.all_gather(pivot_factors, 'col', axis=1, tiled=True).astype(jnp.float32)  91.6 us
    another operation x3, other arithmetic, shards(): lax.linalg.triangular_solve(diag_factor, stacked, left_side=True, lower=T...  84.1 us
    psum x1, waiting for transfers between devices, shards(): m_sum = lax.psum(m_part, 'row')  33.2 us
    another operation x25, local copies, waits for them, and re-layouts  27.8 us
    another operation x15, matrix products, shards(): lax.linalg.triangular_solve(diag_factor, stacked, left_side=True, lower=T...  13.1 us
    another operation x3, other arithmetic, orthonormal_rows(): factor_low = jnp.linalg.cholesky(gram_matrix)  12.4 us
    another operation x2, other arithmetic, orthonormal_rows(): lax.linalg.triangular_solve(factor_low, jnp.swapaxes(sketch_rows, 1, 2),...  10.5 us
  transfers between devices with their start and end apart: 3, of which 3 were waited for; matrix products, arithmetic and copies ran while one was open for 26% of the time, Pallas kernels for 0%

commit v1 on v0

v1 whole, which is shorter than its diff:
```python
import math

import jax
import jax.numpy as jnp
from jax import lax
from jax.experimental import pallas as pl
from jax.experimental.pallas import tpu as pltpu
from jax.sharding import PartitionSpec as P

F32 = jnp.float32
BF16 = jnp.bfloat16
HIGHEST = lax.Precision.HIGHEST
PIECES = 65
SUB = 32
BLOCK = 256


def mm(a, b, ca=1, cb=0, precision=None):
    dims = (((ca,), (cb,)), ((), ()))
    return lax.dot_general(a, b, dims, precision=precision, preferred_element_type=F32)


def split3(x):
    hi = x.astype(BF16)
    rest = x - hi.astype(F32)
    mid = rest.astype(BF16)
    lo = (rest - mid.astype(F32)).astype(BF16)
    return hi, mid, lo


def mixed(a, parts, ca=1, cb=0):
    hi, mid, lo = parts
    return mm(a, lo, ca, cb) + mm(a, mid, ca, cb) + mm(a, hi, ca, cb)


def inverse_cholesky(gram):
    n = gram.shape[0]
    lane = lax.broadcasted_iota(jnp.int32, (8, n), 1)
    row = lax.broadcasted_iota(jnp.int32, (8, n), 0)
    tiles = [gram[8 * t : 8 * t + 8, :] for t in range(n // 8)]
    for k in range(n):
        t0, kk = divmod(k, 8)
        cols = {t: jnp.broadcast_to(tiles[t][:, k : k + 1], (8, n)) for t in range(t0, n // 8)}
        pivot = cols[t0][kk : kk + 1, :]
        here = tiles[t0][kk : kk + 1, :]
        cleared = jnp.where(lane[:1] == k, 1.0, here)
        scaled = cleared / pivot
        head = tiles[t0]
        eliminated = jnp.where(lane == k, 0.0, head) - cols[t0] * scaled
        final = jnp.where(lane <= k, cleared * lax.rsqrt(pivot), 0.0)
        tiles[t0] = jnp.where(row > kk, eliminated, jnp.where(row == kk, final, head))
        for t in range(t0 + 1, n // 8):
            tiles[t] = jnp.where(lane == k, 0.0, tiles[t]) - cols[t] * scaled
    return jnp.concatenate(tiles, axis=0)


def diag_inverse_kernel(d_ref, x_ref):
    n = d_ref.shape[0]
    rank = 128
    blocks = n // rank
    groups = rank // SUB
    lane = lax.broadcasted_iota(jnp.int32, (SUB, rank), 1)
    packed = []
    for b in range(blocks):
        acc = jnp.zeros((SUB, rank), F32)
        for g in range(groups):
            part = d_ref[rank * b + SUB * g : rank * b + SUB * (g + 1), rank * b : rank * (b + 1)]
            acc = jnp.where(lane // SUB == g, part, acc)
        packed.append(acc)
    lane8 = lax.broadcasted_iota(jnp.int32, (8, rank), 1)
    row8 = lax.broadcasted_iota(jnp.int32, (8, rank), 0)
    steps = SUB // 8
    low = [[packed[b][8 * t : 8 * t + 8] for t in range(steps)] for b in range(blocks)]
    inv = [
        [jnp.where(lane8 % SUB == row8 + 8 * t, 1.0, 0.0) for t in range(steps)] for b in range(blocks)
    ]
    for k in range(SUB):
        t0, kk = divmod(k, 8)
        index = (lane8 // SUB) * SUB + k
        for b in range(blocks):
            coef = {t: jnp.take_along_axis(low[b][t], index, axis=1) for t in range(t0, steps)}
            pivot_row = inv[b][t0][kk : kk + 1] / coef[t0][kk : kk + 1]
            head = inv[b][t0]
            head = jnp.where(row8 > kk, head - coef[t0] * pivot_row, head)
            inv[b][t0] = jnp.where(row8 == kk, pivot_row, head)
            for t in range(t0 + 1, steps):
                inv[b][t] = inv[b][t] - coef[t] * pivot_row
    row_full = lax.broadcasted_iota(jnp.int32, (rank, rank), 0)
    lane_full = lax.broadcasted_iota(jnp.int32, (rank, rank), 1)
    whole = []
    for b in range(blocks):
        small = jnp.concatenate(inv[b], axis=0)
        x = jnp.concatenate([jnp.where(lane // SUB == g, small, 0.0) for g in range(groups)], axis=0)
        d = d_ref[rank * b : rank * (b + 1), rank * b : rank * (b + 1)]
        size = SUB
        while size < rank:
            below = ((row_full // size) % 2 == 1) & (lane_full // size == row_full // size - 1)
            off = jnp.where(below, d, 0.0)
            x = x - mm(x, mm(off, x, precision=HIGHEST), precision=HIGHEST)
            size *= 2
        whole.append(x)
    for p in range(blocks // 2):
        first, second = whole[2 * p], whole[2 * p + 1]
        base = BLOCK * p
        off = d_ref[base + rank : base + BLOCK, base : base + rank]
        cross = mm(second, mm(off, first, precision=HIGHEST), precision=HIGHEST)
        x_ref[p, :rank, :rank] = first
        x_ref[p, :rank, rank:] = jnp.zeros((rank, rank), F32)
        x_ref[p, rank:, :rank] = -cross
        x_ref[p, rank:, rank:] = second


def first_kernel(code_ref, row_ref, slot_ref, pivot_ref, a_ref, sketch_ref, y_ref, c_ref):
    rank = sketch_ref.shape[1]
    earlier = pivot_ref.shape[0]
    slots = slot_ref.shape[0]
    sketch = split3(sketch_ref[...])
    weights = [mixed(pivot_ref[j, :, :rank], sketch, 0, 0) for j in range(earlier)]
    kernels = []
    for s in range(slots):
        code = code_ref[s]
        live = code < earlier
        j = jnp.where(live, code, 0)
        coupling = mm(slot_ref[s, :, rank:], pivot_ref[j, :, rank:], 0, 0)
        c_ref[s] = coupling
        weight = weights[0]
        for other in range(1, earlier):
            weight = jnp.where(j == other, weights[other], weight)
        kernels.append(jnp.where(live, mm(coupling, weight, precision=HIGHEST), 0.0))
    left = jnp.concatenate([slot_ref[s, :, :rank] for s in range(slots)], axis=1)
    y_ref[...] = -mixed(left, split3(jnp.concatenate(kernels, axis=0)))
    a_sketch = split3(mixed(a_ref[:, rank:], sketch, 0, 0))
    mine = pl.ds(pl.multiple_of(row_ref[0] * CHUNK, CHUNK), CHUNK)
    y_ref[mine, :] = y_ref[mine, :] + mixed(a_ref[mine, :rank], a_sketch)


def second_kernel(code_ref, row_ref, *refs):
    pieces, (slot_hbm, pivot_hbm, a_hbm, c_ref, basis_ref, m_ref, slot_ref, pivot_ref, a_ref, y_ref, sems) = refs[:PIECES], refs[PIECES:]
    tile, rank = basis_ref.shape
    earlier = pivot_ref.shape[0]
    slots = slot_ref.shape[0]
    pairs = [
        (piece, y_ref.at[pl.ds(start, end - start)])
        for piece, (start, end) in zip(pieces, block_rows(tile))
    ]
    pairs += [(slot_hbm, slot_ref), (pivot_hbm, pivot_ref), (a_hbm, a_ref)]
    loads = [pltpu.make_async_copy(src, dst, sems.at[i]) for i, (src, dst) in enumerate(pairs)]
    for load in loads:
        load.start()
    for load in loads[:PIECES]:
        load.wait()
    y = y_ref[...]
    gram = mm(y, y, 0, 0, HIGHEST)
    q = mm(y, inverse_cholesky(gram), 1, 1, HIGHEST)
    basis_ref[...] = q * math.sqrt(tile)
    parts = split3(q)
    for load in loads[PIECES:]:
        load.wait()
    left = jnp.concatenate([slot_ref[s, :, :rank] for s in range(slots)], axis=1)
    inner = mixed(left, parts, 0, 0)
    lifted = [jnp.zeros((rank, rank), F32) for _ in range(earlier)]
    for s in range(slots):
        code = code_ref[s]
        reduced = mm(c_ref[s], inner[rank * s : rank * (s + 1)], 0, 0, HIGHEST)
        for j in range(earlier):
            lifted[j] = lifted[j] + jnp.where(code == j, reduced, 0.0)
    pivot_left = jnp.concatenate([pivot_ref[j, :, :rank] for j in range(earlier)], axis=1)
    m_ref[...] = -mixed(pivot_left, split3(jnp.concatenate(lifted, axis=0)))
    a_inner = split3(mixed(a_ref[:, :rank], parts, 0, 0))
    mine = pl.ds(pl.multiple_of(row_ref[0] * CHUNK, CHUNK), CHUNK)
    m_ref[mine, :] = m_ref[mine, :] + mixed(a_ref[mine, rank:], a_inner)


def solve_kernel(d_ref, x_ref, *refs):
    pieces, n_ref = refs[:-1], refs[-1]
    tile = n_ref.shape[0]
    m = jnp.concatenate([piece[...] for piece in pieces], axis=0)
    solved = None
    for b in range(tile // BLOCK):
        rows = slice(BLOCK * b, BLOCK * (b + 1))
        right = m[rows]
        if b:
            right = right - mm(d_ref[rows, : BLOCK * b], solved, precision=HIGHEST)
        block = mm(x_ref[b], right, precision=HIGHEST)
        solved = block if solved is None else jnp.concatenate([solved, block], axis=0)
        n_ref[rows, :] = block * (1.0 / math.sqrt(tile))


CHUNK = 64


def call(kernel, out_shape, scalars, far, arrays, loaded=()):
    vmem = pl.BlockSpec(memory_space=pltpu.VMEM)
    scratch = [pltpu.VMEM(x.shape, x.dtype) for x in loaded]
    if far:
        scratch.append(pltpu.SemaphoreType.DMA((len(far),)))
    return pl.pallas_call(
        kernel,
        out_shape=out_shape,
        in_specs=[pl.BlockSpec(memory_space=pltpu.SMEM)] * len(scalars)
        + [pl.BlockSpec(memory_space=pl.ANY)] * len(far)
        + [vmem] * len(arrays),
        out_specs=jax.tree.map(lambda _: vmem, out_shape),
        scratch_shapes=scratch,
        compiler_params=pltpu.CompilerParams(vmem_limit_bytes=(56 if far else 40) * 1024 * 1024),
    )(*scalars, *far, *arrays)


def block_rows(tile):
    tiles = tile // 8
    bounds = [8 * (i * tiles // PIECES) for i in range(PIECES + 1)]
    return list(zip(bounds[:-1], bounds[1:]))


def summed(x):
    return lax.psum(tuple(x[start:end] for start, end in block_rows(x.shape[0])), "row")


def gather_pivot(pivot_factors, cols):
    earlier, depth, width = pivot_factors.shape
    chips = cols // 2
    same_core = [[2 * i + core for i in range(chips)] for core in range(2)]
    same_chip = [[2 * i, 2 * i + 1] for i in range(chips)]
    copies = jnp.broadcast_to(pivot_factors[None], (chips, earlier, depth, width))
    mine = lax.all_to_all(copies, "col", 0, 0, tiled=True, axis_index_groups=same_core)
    other = lax.ppermute(mine, "col", [(i, i ^ 1) for i in range(cols)])
    core = lax.axis_index("col") % 2
    both = jnp.stack([jnp.where(core == 0, mine, other), jnp.where(core == 0, other, mine)], axis=1)
    return jnp.transpose(both, (2, 0, 1, 3, 4)).reshape(earlier, cols * depth, width)


def make(rows, cols):
    def shards(slot_factors, slot_pairs, pivot_factors, a_factors, diag_factor, sketch):
        tile, rank = sketch.shape
        slots = slot_factors.shape[2]
        whole = jax.ShapeDtypeStruct((tile, rank), F32)
        codes = slot_pairs.reshape(slots)
        row = lax.axis_index("row").astype(jnp.int32).reshape(1)
        slot_data = slot_factors[0, 0]
        a_data = a_factors[0]
        inverse_shape = jax.ShapeDtypeStruct((tile // BLOCK, BLOCK, BLOCK), F32)
        inverse = call(diag_inverse_kernel, inverse_shape, (), (), (diag_factor,))
        pivot = gather_pivot(pivot_factors, cols)
        y_part, coupling = call(
            first_kernel,
            (whole, jax.ShapeDtypeStruct((slots, rank, rank), F32)),
            (codes, row),
            (),
            (slot_data, pivot, a_data, sketch),
        )
        basis, m_part = call(
            second_kernel,
            (whole, whole),
            (codes, row),
            (*summed(y_part), slot_data, pivot, a_data),
            (coupling,),
            (slot_data, pivot, a_data, whole),
        )
        coefficient = call(solve_kernel, whole, (), (), (diag_factor, inverse, *summed(m_part)))
        return basis[None], coefficient[None]

    return shards


def solution(mesh):
    in_specs = (
        P("row", "col", None, None, None),
        P("row", "col", None),
        P("row", "col", None),
        P("col", None, None),
        P(),
        P(),
    )
    out_specs = (P("col", None, None), P("col", None, None))
    body = make(mesh.shape["row"], mesh.shape["col"])
    return jax.shard_map(body, mesh=mesh, in_specs=in_specs, out_specs=out_specs, check_vma=False)
```

time: 456 us -> 208 us (0.46)
  waiting for transfers between devices: 268 us -> 0.01 us
  blocking collectives: 0 us -> 162 us
  other arithmetic: 110 us -> 1.35 us
  matrix products: 31.9 us -> 0 us
  Pallas kernels: 0 us -> 31 us
  local copies, waits for them, and re-layouts: 31.4 us -> 10.2 us
  between operations: 14.1 us -> 0.84 us
    psum x2 -> x0, waiting for transfers between devices: 175 us -> none  [the longest x1 142 us: shards(): sketch_rows = y_a - lax.psum(y_part, 'row')]
    psum x0 -> x2, blocking collectives: none -> 134 us  [summed(): lax.psum(tuple((x[start:end] for start, end in block_rows(x.shape[0]))),...]
    another operation x9 -> x1, other arithmetic: 108 us -> 1.25 us  [gather_pivot(): jnp.stack([jnp.where(core == 0, mine, other), jnp.where(core == 0, other,...]
    all_gather x1 -> x0, waiting for transfers between devices: 91.6 us -> none  [shards(): lax.all_gather(pivot_factors, 'col', axis=1, tiled=True).astype(jnp.float32)]
    pallas_call x0 -> x4, Pallas kernels: none -> 31 us  [call(): pl.pallas_call(kernel, out_shape=out_shape, in_specs=[pl.BlockSpec(memory...]
    all_to_all x0 -> x1, blocking collectives: none -> 28.5 us  [gather_pivot(): lax.all_to_all(copies, 'col', 0, 0, tiled=True, axis_index_groups=same_core)]
    another operation x27 -> x0, local copies, waits for them, and re-layouts: 27.8 us -> none
    dot_general x16 -> x0, matrix products: 18.2 us -> none  [the longest x1 2.73 us: shards(): jnp.einsum('st,sbd->tbd', tile_selector, lifted, precision=precise_mode)]
  transfers between devices with their start and end apart: 3 -> 1, of which waited for: 3 -> 0; matrix products, arithmetic and copies ran while one was open for 26% -> 0% of each run, Pallas kernels for 0% -> 3%
where the time goes in v1:
time: 208 us; the launch traced here: 207 us
  blocking collectives  162 us (78%)
  Pallas kernels  31 us (15%)
  local copies, waits for them, and re-layouts  10.2 us (5%)
    psum x2, blocking collectives, summed(): lax.psum(tuple((x[start:end] for start, end in block_rows(x.shape[0]))),...  134 us
    pallas_call x4, Pallas kernels, call(): pl.pallas_call(kernel, out_shape=out_shape, in_specs=[pl.BlockSpec(memory...  31 us
    all_to_all x1, blocking collectives, gather_pivot(): lax.all_to_all(copies, 'col', 0, 0, tiled=True, axis_index_groups=same_core)  28.5 us
    unnamed x16, local copies, waits for them, and re-layouts  5.03 us
    slice x10, local copies, waits for them, and re-layouts, summed(): x[start:end]  4.24 us
  transfers between devices with their start and end apart: 1, of which 0 were waited for; matrix products, arithmetic and copies ran while one was open for 0% of the time, Pallas kernels for 3%

profile of v1, /device:TPU:6, one launch (start us, length us, event | category | flops | bytes accessed | tf_op | source)
XLA Modules:
  0.0 207.3 jit_solution(2177084530887995339)
XLA Ops:
  0.6 0.8 broadcast_in_dim.12
  1.4 28.5 %all_to_all.5 = bf16[32,2,16,256]{3,2,1,0:T(8,128)(2,1)S(1)} all-to-all(bf16[32,2,16,256]{3,2,1,0:T(8,128)(2,1)S(1)} %broadcast_in_dim.12), channel_id=1, replica_groups={{0,2,4,6,8,10,12,14,16,18,20,22,24,26,28,30,32,34,36,38,40,42,44,46,48,..., dimensions={0} | all-to-all | bytes 1048576 | tf_op jit(solution)/shard_map/all_to_all | solution.py:225
  29.9 1.9 collective-permute-start
  31.8 0.0 copy-start
  31.8 2.2 %copy-done = f32[1024,1024]{1,0:T(8,128)S(1)} copy-done((f32[1024,1024]{1,0:T(8,128)S(1)}, f32[1024,1024]{1,0:T(8,128)}, u32[]{:S(2)}) %copy-start) | copy-done | bytes 4194328
  34.0 5.4 %shard_map.79.x_ref = f32[4,256,256]{2,1,0:T(8,128)S(1)} custom-call(f32[1024,1024]{1,0:T(8,128)S(1)} %copy-done), custom_call_target="tpu_custom_call" | custom-call | tf_op jit(solution)/shard_map/pallas_call | solution.py:197
  39.4 0.0 copy-start.3
  39.4 0.0 copy-start.4
  39.4 0.0 copy-start.5
  39.4 0.0 copy-start.7
  39.4 0.0 collective-permute-done
  39.4 1.3 select_bitcast_fusion.1
  40.7 0.1 maximum_bitcast_fusion
  40.8 0.1 copy.9
  41.0 0.0 copy-start.2
  41.0 0.0 copy-done.3
  41.0 0.0 copy-done.4
  41.0 0.1 copy-done.5
  41.1 0.0 copy-done.7
  41.1 2.5 %shard_map.77 = (f32[1024,128]{1,0:T(8,128)S(1)}, f32[2,128,128]{2,1,0:T(8,128)S(1)}) custom-call(s32[2]{0:T(128)S(1)} %bitcast.20, s32[1]{0:T(128)} %bitcast.1.row_ref, bf16[2,1024,256]{2,1,0:T(8,128)(2,1)S(1)} %bitcast.16, bf16[2,1024,256]{2,1,0:T(8,128)(2,1)S(1)} %bitcast.13, bf16[1024,256]{1,0:T(8,128)(2,1)S(1)} %bitcast.18, f32[1024,128]{1,0:T(8,128)S(1)} %copy-done.5), custom_call_target="tpu_custom_call" | custom-call | tf_op jit(solution)/shard_map/pallas_call | solution.py:197
  43.7 0.6 copy-done.6
  44.3 74.0 %all-reduce.4 = (f32[8,128]{1,0:T(8,128)}, f32[16,128]{1,0:T(8,128)}, f32[16,128]{1,0:T(8,128)}, f32[16,128]{1,0:T(8,128)}, f32[16,128]{1,0:T(8,128)}, /*index=5...) all-reduce(f32[8,128]{1,0:T(8,128)S(1)} %get-tuple-element.246, ...), channel_id=1, replica_groups=mesh['row'=16,'col'=64] {'row'}, use_global_device_ids=true, to_apply=%region_0.1 | all-reduce | flops 131072 | bytes 1048576 | tf_op jit(solution)/shard_map/psum | solution.py:216
  118.3 17.9 %shard_map.78 = (f32[1024,128]{1,0:T(8,128)}, f32[1024,128]{1,0:T(8,128)}) custom-call(s32[2]{0:T(128)} %bitcast.19, s32[1]{0:T(128)} %bitcast.1.row_ref, f32[8,128]{1,0:T(8,128)} %get-tuple-element.75.refs_0_, f32[16,128]{1,0:T(8,128)} %get-tuple-element.76.refs_1_, f32[16,128]{1,0:T(8,128)} %get-tuple-element.77.refs_2_, ...), custom_call_target="tpu_custom_call" | custom-call | tf_op jit(solution)/shard_map/pallas_call | solution.py:197
  136.2 0.7 fusion.2
  136.9 0.8 fusion.4
  137.7 0.9 fusion.3
  138.6 0.9 fusion
  139.5 0.9 fusion.1
  140.4 59.6 %all-reduce.5 = (f32[8,128]{1,0:T(8,128)S(1)}, f32[16,128]{1,0:T(8,128)S(1)}, f32[16,128]{1,0:T(8,128)S(1)}, f32[16,128]{1,0:T(8,128)S(1)}, f32[16,128]{1,0:T(8,...) all-reduce(f32[8,128]{1,0:T(8,128)S(1)} %get-tuple-element.181, ...), channel_id=1, replica_groups=mesh['row'=16,'col'=64] {'row'}, use_global_device_ids=true, to_apply=%region_65.66 | all-reduce | flops 131072 | bytes 1048576 | tf_op jit(solution)/shard_map/psum | solution.py:216
  199.9 0.0 copy-start.1
  200.0 2.2 %copy-done.1 = f32[1024,1024]{1,0:T(8,128)S(1)} copy-done((f32[1024,1024]{1,0:T(8,128)S(1)}, f32[1024,1024]{1,0:T(8,128)}, u32[]{:S(2)}) %copy-start.1) | copy-done | bytes 4194328
  202.1 5.2 %shard_map.80 = f32[1024,128]{1,0:T(8,128)} custom-call(f32[1024,1024]{1,0:T(8,128)S(1)} %copy-done.1, f32[4,256,256]{2,1,0:T(8,128)S(1)} %shard_map.79.x_ref, f32[8,128]{1,0:T(8,128)S(1)} %get-tuple-element.10.refs_0_, f32[16,128]{1,0:T(8,128)S(1)} %get-tuple-element.11.refs_1_, f32[16,128]{1,0:T(8,128)S(1)} %get-tuple-element.12.refs_2_, ...), custom_call_target="tpu_custom_call" | custom-call | tf_op jit(solution)/shard_map/pallas_call | solution.py:197
  (7 shorter events, 0.1 us)
Async XLA Ops:
  29.9 9.6 %collective-permute-start = (bf16[32,2,16,256]{3,2,1,0:T(8,128)(2,1)S(1)}, bf16[32,2,16,256]{3,2,1,0:T(8,128)(2,1)}, u32[]{:S(2)}, u32[]{:S(2)}) collective-permute-start(bf16[32,2,16,256]{3,2,1,0:T(8,128)(2,1)S(1)} %all_to_all.5), channel_id=1, source_target_pairs={{0,1},{1,0},{2,3},{3,2},{4,5},{5,4},{6,7},{7,6},{8,9},{9,8},{10,11... | collective-permute-start | bytes 1572872 | tf_op jit(solution)/shard_map/ppermute | solution.py:226
  31.8 2.2 %copy-start = (f32[1024,1024]{1,0:T(8,128)S(1)}, f32[1024,1024]{1,0:T(8,128)}, u32[]{:S(2)}) copy-start(f32[1024,1024]{1,0:T(8,128)} %d_ref.3) | copy-start | bytes 12582916
  39.4 1.6 copy-start.3
  39.4 1.6 copy-start.4
  39.4 1.7 copy-start.5
  39.4 1.6 copy-start.7
  41.0 77.3 %copy-start.2 = (bf16[2,32,2,16,256]{4,3,2,1,0:T(8,128)(2,1)}, bf16[2,32,2,16,256]{4,3,2,1,0:T(8,128)(2,1)S(1)}, u32[]{:S(2)}) copy-start(bf16[2,32,2,16,256]{4,3,2,1,0:T(8,128)(2,1)S(1)} %copy.9) | copy-start | bytes 3145732
  43.6 0.7 copy-start.6
  199.9 2.2 %copy-start.1 = (f32[1024,1024]{1,0:T(8,128)S(1)}, f32[1024,1024]{1,0:T(8,128)}, u32[]{:S(2)}) copy-start(f32[1024,1024]{1,0:T(8,128)} %d_ref.3) | copy-start | bytes 12582916

commit v2 on v1

--- a/solution.py
+++ b/solution.py
@@ -33,29 +33,68 @@
     return mm(a, lo, ca, cb) + mm(a, mid, ca, cb) + mm(a, hi, ca, cb)
 
 
+def mm3(a, b):
+    (a_hi, a_lo, _), (b_hi, b_lo, _) = split3(a), split3(b)
+    return mm(a_lo, b_hi) + mm(a_hi, b_lo) + mm(a_hi, b_hi)
+
+
 def inverse_cholesky(gram):
     n = gram.shape[0]
-    lane = lax.broadcasted_iota(jnp.int32, (8, n), 1)
-    row = lax.broadcasted_iota(jnp.int32, (8, n), 0)
+    wide = (8, n)
+    lane = lax.broadcasted_iota(jnp.int32, wide, 1)
+    row = lax.broadcasted_iota(jnp.int32, wide, 0)
     tiles = [gram[8 * t : 8 * t + 8, :] for t in range(n // 8)]
-    for k in range(n):
-        t0, kk = divmod(k, 8)
-        cols = {t: jnp.broadcast_to(tiles[t][:, k : k + 1], (8, n)) for t in range(t0, n // 8)}
-        pivot = cols[t0][kk : kk + 1, :]
-        here = tiles[t0][kk : kk + 1, :]
-        cleared = jnp.where(lane[:1] == k, 1.0, here)
-        scaled = cleared / pivot
-        head = tiles[t0]
-        eliminated = jnp.where(lane == k, 0.0, head) - cols[t0] * scaled
-        final = jnp.where(lane <= k, cleared * lax.rsqrt(pivot), 0.0)
-        tiles[t0] = jnp.where(row > kk, eliminated, jnp.where(row == kk, final, head))
-        for t in range(t0 + 1, n // 8):
-            tiles[t] = jnp.where(lane == k, 0.0, tiles[t]) - cols[t] * scaled
+    for p in range(n // 8):
+        inside = lane // 8 == p
+        head = tiles[p]
+        columns = [jnp.broadcast_to(head[:, 8 * p + j : 8 * p + j + 1], wide) for j in range(8)]
+        square = [[jnp.broadcast_to(columns[j][i : i + 1, :], wide) for j in range(i + 1)] for i in range(8)]
+        rows = [
+            jnp.where(inside, jnp.where(lane == 8 * p + i, 1.0, 0.0), jnp.broadcast_to(head[i : i + 1, :], wide))
+            for i in range(8)
+        ]
+        ratios, inverses = {}, []
+        for j in range(8):
+            inverses.append(1.0 / square[j][j])
+            below = [square[i][j] for i in range(8)[j + 1 :]]
+            for i in range(j + 1, 8):
+                ratios[i, j] = square[i][j] * inverses[j]
+                for m in range(j + 1, i + 1):
+                    square[i][m] = square[i][m] - ratios[i, j] * below[m - j - 1]
+                rows[i] = rows[i] - ratios[i, j] * rows[j]
+        solved = [None] * 8
+        for i in reversed(range(8)):
+            solved[i] = rows[i] * inverses[i]
+            for j in range(i + 1, 8):
+                solved[i] = solved[i] - ratios[j, i] * solved[j]
+        final = rows[0] * lax.rsqrt(square[0][0])
+        for i in range(1, 8):
+            final = jnp.where(row == i, rows[i] * lax.rsqrt(square[i][i]), final)
+        tiles[p] = jnp.where(lane <= row + 8 * p, final, 0.0)
+        for t in range(p + 1, n // 8):
+            old = tiles[t]
+            terms = [jnp.broadcast_to(old[:, 8 * p + i : 8 * p + i + 1], wide) * solved[i] for i in range(8)]
+            while len(terms) > 1:
+                terms = [a + b for a, b in zip(terms[::2], terms[1::2])]
+            tiles[t] = jnp.where(inside, 0.0, old) - terms[0]
     return jnp.concatenate(tiles, axis=0)
 
 
-def diag_inverse_kernel(d_ref, x_ref):
-    n = d_ref.shape[0]
+def diag_inverse_kernel(d_hbm, x_ref, d_ref, sems):
+    n = d_hbm.shape[0]
+    loads = []
+    for p in range(n // BLOCK):
+        part = pl.ds(BLOCK * p, BLOCK)
+        loads.append(pltpu.make_async_copy(d_hbm.at[part, part], d_ref.at[part], sems.at[p]))
+    for load in loads:
+        load.start()
+    for load in loads:
+        load.wait()
+
+    def block(start, size, column, width):
+        base = start // BLOCK * BLOCK
+        return d_ref[start : start + size, column - base : column - base + width]
+
     rank = 128
     blocks = n // rank
     groups = rank // SUB
@@ -64,7 +103,7 @@
     for b in range(blocks):
         acc = jnp.zeros((SUB, rank), F32)
         for g in range(groups):
-            part = d_ref[rank * b + SUB * g : rank * b + SUB * (g + 1), rank * b : rank * (b + 1)]
+            part = block(rank * b + SUB * g, SUB, rank * b, rank)
             acc = jnp.where(lane // SUB == g, part, acc)
         packed.append(acc)
     lane8 = lax.broadcasted_iota(jnp.int32, (8, rank), 1)
@@ -91,19 +130,19 @@
     for b in range(blocks):
         small = jnp.concatenate(inv[b], axis=0)
         x = jnp.concatenate([jnp.where(lane // SUB == g, small, 0.0) for g in range(groups)], axis=0)
-        d = d_ref[rank * b : rank * (b + 1), rank * b : rank * (b + 1)]
+        d = block(rank * b, rank, rank * b, rank)
         size = SUB
         while size < rank:
             below = ((row_full // size) % 2 == 1) & (lane_full // size == row_full // size - 1)
             off = jnp.where(below, d, 0.0)
-            x = x - mm(x, mm(off, x, precision=HIGHEST), precision=HIGHEST)
+            x = x - mm3(x, mm3(off, x))
             size *= 2
         whole.append(x)
     for p in range(blocks // 2):
         first, second = whole[2 * p], whole[2 * p + 1]
         base = BLOCK * p
-        off = d_ref[base + rank : base + BLOCK, base : base + rank]
-        cross = mm(second, mm(off, first, precision=HIGHEST), precision=HIGHEST)
+        off = block(base + rank, rank, base, rank)
+        cross = mm3(second, mm3(off, first))
         x_ref[p, :rank, :rank] = first
         x_ref[p, :rank, rank:] = jnp.zeros((rank, rank), F32)
         x_ref[p, rank:, :rank] = -cross
@@ -135,7 +174,9 @@
 
 
 def second_kernel(code_ref, row_ref, *refs):
-    pieces, (slot_hbm, pivot_hbm, a_hbm, c_ref, basis_ref, m_ref, slot_ref, pivot_ref, a_ref, y_ref, sems) = refs[:PIECES], refs[PIECES:]
+    pieces, outs = refs[:PIECES], refs[PIECES + 5 : 2 * PIECES + 5]
+    slot_hbm, pivot_hbm, a_hbm, c_hbm, basis_ref = refs[PIECES : PIECES + 5]
+    slot_ref, pivot_ref, a_ref, c_ref, y_ref, sems = refs[2 * PIECES + 5 :]
     tile, rank = basis_ref.shape
     earlier = pivot_ref.shape[0]
     slots = slot_ref.shape[0]
@@ -143,7 +184,7 @@
         (piece, y_ref.at[pl.ds(start, end - start)])
         for piece, (start, end) in zip(pieces, block_rows(tile))
     ]
-    pairs += [(slot_hbm, slot_ref), (pivot_hbm, pivot_ref), (a_hbm, a_ref)]
+    pairs += [(slot_hbm, slot_ref), (pivot_hbm, pivot_ref), (a_hbm, a_ref), (c_hbm, c_ref)]
     loads = [pltpu.make_async_copy(src, dst, sems.at[i]) for i, (src, dst) in enumerate(pairs)]
     for load in loads:
         load.start()
@@ -165,44 +206,68 @@
         for j in range(earlier):
             lifted[j] = lifted[j] + jnp.where(code == j, reduced, 0.0)
     pivot_left = jnp.concatenate([pivot_ref[j, :, :rank] for j in range(earlier)], axis=1)
-    m_ref[...] = -mixed(pivot_left, split3(jnp.concatenate(lifted, axis=0)))
+    y_ref[...] = -mixed(pivot_left, split3(jnp.concatenate(lifted, axis=0)))
     a_inner = split3(mixed(a_ref[:, :rank], parts, 0, 0))
     mine = pl.ds(pl.multiple_of(row_ref[0] * CHUNK, CHUNK), CHUNK)
-    m_ref[mine, :] = m_ref[mine, :] + mixed(a_ref[mine, rank:], a_inner)
-
-
-def solve_kernel(d_ref, x_ref, *refs):
-    pieces, n_ref = refs[:-1], refs[-1]
+    y_ref[mine, :] = y_ref[mine, :] + mixed(a_ref[mine, rank:], a_inner)
+    stores = [
+        pltpu.make_async_copy(y_ref.at[pl.ds(start, end - start)], out, sems.at[i])
+        for i, (out, (start, end)) in enumerate(zip(outs, block_rows(tile)))
+    ]
+    for store in stores:
+        store.start()
+    for store in stores:
+        store.wait()
+
+
+def solve_kernel(d_hbm, x_hbm, *refs):
+    pieces, (n_ref, d_ref, x_ref, m_ref, sems) = refs[:PIECES], refs[PIECES:]
     tile = n_ref.shape[0]
-    m = jnp.concatenate([piece[...] for piece in pieces], axis=0)
-    solved = None
-    for b in range(tile // BLOCK):
+    count = tile // BLOCK
+    takes = [
+        pltpu.make_async_copy(piece, m_ref.at[pl.ds(start, end - start)], sems.at[i + count])
+        for i, (piece, (start, end)) in enumerate(zip(pieces, block_rows(tile)))
+    ]
+    takes.append(pltpu.make_async_copy(x_hbm, x_ref, sems.at[0]))
+    for take in takes:
+        take.start()
+    loads = []
+    for b in range(1, count):
+        part = pl.ds(BLOCK * b, BLOCK), pl.ds(0, BLOCK * b)
+        loads.append(pltpu.make_async_copy(d_hbm.at[part], d_ref.at[part], sems.at[b]))
+    for load in loads:
+        load.start()
+    for take in takes:
+        take.wait()
+    m = m_ref[...]
+    solved = []
+    for b in range(count):
         rows = slice(BLOCK * b, BLOCK * (b + 1))
         right = m[rows]
         if b:
-            right = right - mm(d_ref[rows, : BLOCK * b], solved, precision=HIGHEST)
-        block = mm(x_ref[b], right, precision=HIGHEST)
-        solved = block if solved is None else jnp.concatenate([solved, block], axis=0)
-        n_ref[rows, :] = block * (1.0 / math.sqrt(tile))
+            loads[b - 1].wait()
+            right = right - mm3(d_ref[rows, : BLOCK * b], jnp.concatenate(solved, axis=0))
+        solved.append(mm3(x_ref[b], right))
+        n_ref[rows, :] = solved[b] * (1.0 / math.sqrt(tile))
 
 
 CHUNK = 64
 
 
-def call(kernel, out_shape, scalars, far, arrays, loaded=()):
+def call(kernel, out_shape, scalars, far, arrays, loaded=(), grant=56, blocks=()):
     vmem = pl.BlockSpec(memory_space=pltpu.VMEM)
     scratch = [pltpu.VMEM(x.shape, x.dtype) for x in loaded]
     if far:
-        scratch.append(pltpu.SemaphoreType.DMA((len(far),)))
+        scratch.append(pltpu.SemaphoreType.DMA((len(far) + 8,)))
     return pl.pallas_call(
         kernel,
-        out_shape=out_shape,
+        out_shape=[*out_shape, *blocks],
         in_specs=[pl.BlockSpec(memory_space=pltpu.SMEM)] * len(scalars)
         + [pl.BlockSpec(memory_space=pl.ANY)] * len(far)
         + [vmem] * len(arrays),
-        out_specs=jax.tree.map(lambda _: vmem, out_shape),
+        out_specs=[vmem] * len(out_shape) + [pl.BlockSpec(memory_space=pl.ANY)] * len(blocks),
         scratch_shapes=scratch,
-        compiler_params=pltpu.CompilerParams(vmem_limit_bytes=(56 if far else 40) * 1024 * 1024),
+        compiler_params=pltpu.CompilerParams(vmem_limit_bytes=grant * 1024 * 1024),
     )(*scalars, *far, *arrays)
 
 
@@ -212,8 +277,8 @@
     return list(zip(bounds[:-1], bounds[1:]))
 
 
-def summed(x):
-    return lax.psum(tuple(x[start:end] for start, end in block_rows(x.shape[0])), "row")
+def summed(blocks):
+    return lax.psum(tuple(blocks), "row")
 
 
 def gather_pivot(pivot_factors, cols):
@@ -239,24 +304,41 @@
         slot_data = slot_factors[0, 0]
         a_data = a_factors[0]
         inverse_shape = jax.ShapeDtypeStruct((tile // BLOCK, BLOCK, BLOCK), F32)
-        inverse = call(diag_inverse_kernel, inverse_shape, (), (), (diag_factor,))
+        diagonal = jax.ShapeDtypeStruct((tile, BLOCK), F32)
+        blocks = [jax.ShapeDtypeStruct((end - start, rank), F32) for start, end in block_rows(tile)]
+        (inverse,) = call(diag_inverse_kernel, [inverse_shape], (), (diag_factor,), (), (diagonal,))
         pivot = gather_pivot(pivot_factors, cols)
         y_part, coupling = call(
             first_kernel,
-            (whole, jax.ShapeDtypeStruct((slots, rank, rank), F32)),
+            [whole, jax.ShapeDtypeStruct((slots, rank, rank), F32)],
             (codes, row),
             (),
             (slot_data, pivot, a_data, sketch),
+            grant=40,
         )
-        basis, m_part = call(
+        basis, *m_part = call(
             second_kernel,
-            (whole, whole),
+            [whole],
             (codes, row),
-            (*summed(y_part), slot_data, pivot, a_data),
-            (coupling,),
-            (slot_data, pivot, a_data, whole),
+            (
+                *summed(y_part[start:end] for start, end in block_rows(tile)),
+                slot_data,
+                pivot,
+                a_data,
+                coupling,
+            ),
+            (),
+            (slot_data, pivot, a_data, coupling, whole),
+            blocks=blocks,
         )
-        coefficient = call(solve_kernel, whole, (), (), (diag_factor, inverse, *summed(m_part)))
+        (coefficient,) = call(
+            solve_kernel,
+            [whole],
+            (),
+            (diag_factor, inverse, *summed(m_part)),
+            (),
+            (diag_factor, inverse_shape, whole),
+        )
         return basis[None], coefficient[None]
 
     return shards

time: 208 us -> 197 us (0.947)
  local copies, waits for them, and re-layouts: 10.2 us -> 2.98 us
  Pallas kernels: 31 us -> 27.7 us
    slice x10 -> x5, local copies, waits for them, and re-layouts: 4.24 us -> 0.06 us  [shards(): y_part[start:end]]
    pallas_call x4, Pallas kernels: 31 us -> 27.7 us  [call(): pl.pallas_call(kernel, out_shape=[*out_shape, *blocks], in_specs=[pl.Bloc...]
    unnamed x16 -> x12, local copies, waits for them, and re-layouts: 5.03 us -> 2.01 us
where the time goes in v2:
time: 197 us; the launch traced here: 196 us
  blocking collectives  163 us (83%)
  Pallas kernels  27.7 us (14%)
  local copies, waits for them, and re-layouts  2.98 us (2%)
    psum x2, blocking collectives, summed(): return lax.psum(tuple(blocks), 'row')  134 us
    all_to_all x1, blocking collectives, gather_pivot(): lax.all_to_all(copies, 'col', 0, 0, tiled=True, axis_index_groups=same_core)  28.5 us
    pallas_call x4, Pallas kernels, call(): pl.pallas_call(kernel, out_shape=[*out_shape, *blocks], in_specs=[pl.Bloc...  27.7 us
  transfers between devices with their start and end apart: 1, of which 0 were waited for; matrix products, arithmetic and copies ran while one was open for 0% of the time, Pallas kernels for 3%

profile of v2, /device:TPU:6, one launch (start us, length us, event | category | flops | bytes accessed | tf_op | source)
XLA Modules:
  0.0 196.4 jit_solution(11310616614524899248)
XLA Ops:
  0.6 0.8 broadcast_in_dim.12
  1.4 28.5 %all_to_all.5 = bf16[32,2,16,256]{3,2,1,0:T(8,128)(2,1)S(1)} all-to-all(bf16[32,2,16,256]{3,2,1,0:T(8,128)(2,1)S(1)} %broadcast_in_dim.12), channel_id=1, replica_groups={{0,2,4,6,8,10,12,14,16,18,20,22,24,26,28,30,32,34,36,38,40,42,44,46,48,..., dimensions={0} | all-to-all | bytes 1048576 | tf_op jit(solution)/shard_map/all_to_all | solution.py:290
  29.9 1.9 collective-permute-start
  31.8 6.3 %shard_map.79.x_hbm = f32[4,256,256]{2,1,0:T(8,128)} custom-call(f32[1024,1024]{1,0:T(8,128)} %d_hbm.3), custom_call_target="tpu_custom_call" | custom-call | tf_op jit(solution)/shard_map/pallas_call | solution.py:262
  38.1 0.0 copy-start.1
  38.1 0.0 copy-start.2
  38.1 0.0 copy-start.3
  38.1 0.0 copy-start.5
  38.1 0.0 collective-permute-done
  38.1 0.1 select_bitcast_fusion.1
  38.3 0.1 maximum_bitcast_fusion
  38.4 0.1 copy.9
  38.5 0.0 copy-start
  38.5 0.8 copy-done.1
  39.3 0.1 copy-done.2
  39.4 0.5 copy-done.3
  40.0 0.0 copy-done.5
  40.0 2.5 %shard_map.77 = (f32[1024,128]{1,0:T(8,128)S(1)}, f32[2,128,128]{2,1,0:T(8,128)S(1)}) custom-call(s32[2]{0:T(128)S(1)} %bitcast.20, s32[1]{0:T(128)} %bitcast.1.row_ref, bf16[2,1024,256]{2,1,0:T(8,128)(2,1)S(1)} %bitcast.16, bf16[2,1024,256]{2,1,0:T(8,128)(2,1)S(1)} %bitcast.13, bf16[1024,256]{1,0:T(8,128)(2,1)S(1)} %bitcast.18, f32[1024,128]{1,0:T(8,128)S(1)} %copy-done.3), custom_call_target="tpu_custom_call" | custom-call | tf_op jit(solution)/shard_map/pallas_call | solution.py:262
  42.5 0.0 copy-start.4
  42.6 0.6 copy-done.4
  43.2 74.0 %all-reduce.4 = (f32[8,128]{1,0:T(8,128)}, f32[16,128]{1,0:T(8,128)}, f32[16,128]{1,0:T(8,128)}, f32[16,128]{1,0:T(8,128)}, f32[16,128]{1,0:T(8,128)}, /*index=5...) all-reduce(f32[8,128]{1,0:T(8,128)S(1)} %get-tuple-element.309, ...), channel_id=1, replica_groups=mesh['row'=16,'col'=64] {'row'}, use_global_device_ids=true, to_apply=%region_0.1 | all-reduce | flops 131072 | bytes 1048576 | tf_op jit(solution)/shard_map/psum | solution.py:281
  117.2 0.0 copy-done
  117.2 13.5 %shard_map.78 = (f32[1024,128]{1,0:T(8,128)}, f32[8,128]{1,0:T(8,128)}, f32[16,128]{1,0:T(8,128)}, f32[16,128]{1,0:T(8,128)}, f32[16,128]{1,0:T(8,128)}, /*index...) custom-call(s32[2]{0:T(128)} %bitcast.19, ...), custom_call_target="tpu_custom_call" | custom-call | tf_op jit(solution)/shard_map/pallas_call | solution.py:262
  130.7 60.1 %all-reduce.5 = (f32[8,128]{1,0:T(8,128)}, f32[16,128]{1,0:T(8,128)}, f32[16,128]{1,0:T(8,128)}, f32[16,128]{1,0:T(8,128)}, f32[16,128]{1,0:T(8,128)}, /*index=5...) all-reduce(f32[8,128]{1,0:T(8,128)} %get-tuple-element.73, ...), channel_id=1, replica_groups=mesh['row'=16,'col'=64] {'row'}, use_global_device_ids=true, to_apply=%region_65.66 | all-reduce | flops 131072 | bytes 1048576 | tf_op jit(solution)/shard_map/psum | solution.py:281
  190.8 5.4 %shard_map.80 = f32[1024,128]{1,0:T(8,128)} custom-call(f32[1024,1024]{1,0:T(8,128)} %d_hbm.3, f32[4,256,256]{2,1,0:T(8,128)} %shard_map.79.x_hbm, f32[8,128]{1,0:T(8,128)} %get-tuple-element.138.refs_0_, f32[16,128]{1,0:T(8,128)} %get-tuple-element.139.refs_1_, f32[16,128]{1,0:T(8,128)} %get-tuple-element.140.refs_2_, ...), custom_call_target="tpu_custom_call" | custom-call | tf_op jit(solution)/shard_map/pallas_call | solution.py:262
  (5 shorter events, 0.1 us)
Async XLA Ops:
  29.9 8.3 %collective-permute-start = (bf16[32,2,16,256]{3,2,1,0:T(8,128)(2,1)S(1)}, bf16[32,2,16,256]{3,2,1,0:T(8,128)(2,1)S(1)}, u32[]{:S(2)}, u32[]{:S(2)}) collective-permute-start(bf16[32,2,16,256]{3,2,1,0:T(8,128)(2,1)S(1)} %all_to_all.5), channel_id=1, source_target_pairs={{0,1},{1,0},{2,3},{3,2},{4,5},{5,4},{6,7},{7,6},{8,9},{9,8},{10,11... | collective-permute-start | bytes 1572872 | tf_op jit(solution)/shard_map/ppermute | solution.py:291
  38.1 1.2 copy-start.1
  38.1 1.3 copy-start.2
  38.1 1.9 copy-start.3
  38.1 1.9 copy-start.5
  38.5 78.6 %copy-start = (bf16[2,32,2,16,256]{4,3,2,1,0:T(8,128)(2,1)}, bf16[2,32,2,16,256]{4,3,2,1,0:T(8,128)(2,1)S(1)}, u32[]{:S(2)}) copy-start(bf16[2,32,2,16,256]{4,3,2,1,0:T(8,128)(2,1)S(1)} %copy.9) | copy-start | bytes 3145732
  42.5 0.7 copy-start.4
